TPU v7x, 32 devices: a whole 2x2x4 slice. The times are simulated.
32 devices in a mesh: cfg: 2 (over core), seq: 8 (over z, x), wt: 2 (over y).
Axes of the slice: x: 2, y: 2, z: 4, core: 2. Of those that a mesh axis runs over, the one named last changes fastest.
Arguments:
- hidden: bfloat16 [2, 1280, 5120], P('cfg', 'seq'), may hold values from -1.5 to 1.5
- latent: float32 [1280, 64], P('seq', 'cfg'), may hold values from -6 to 6
- tenant_lengths: int32 [4], replicated, may hold values from 1 to 960, 1280 in all
- grid_positions: int32 [1280, 3], P('seq'), may hold values from 0 to 47
- text_kv: bfloat16 [2, 2, 2048, 3072], P(None, 'cfg', None, 'wt'), may hold values from -6 to 6
- text_lengths: int32 [2, 4], P('cfg'), may hold values from 1 to 512
- w_query: bfloat16 [5120, 3072], P(('cfg', 'seq'), 'wt'), may hold values from -0.078125 to 0.078125
- w_key: bfloat16 [5120, 3072], P(('cfg', 'seq'), 'wt'), may hold values from -0.078125 to 0.078125
- w_value: bfloat16 [5120, 3072], P(('cfg', 'seq'), 'wt'), may hold values from -0.078125 to 0.078125
- w_out: bfloat16 [5120, 3072], P(('cfg', 'seq'), 'wt'), may hold values from -0.109375 to 0.109375
- w_cross_query: bfloat16 [5120, 3072], P(('cfg', 'seq'), 'wt'), may hold values from -0.078125 to 0.078125
- w_cross_out: bfloat16 [5120, 3072], P(('cfg', 'seq'), 'wt'), may hold values from -0.109375 to 0.109375
- w_head: bfloat16 [5120, 64], replicated, may hold values from -0.078125 to 0.078125
- guidance: float32 [1], replicated, may hold values from 3 to 7
- step_size: float32 [1], replicated, may hold values from -0.3 to -0.05
Outputs:
- hidden_out: bfloat16 [2, 1280, 5120], P('cfg', 'seq', 'wt')
- latent_next: float32 [1280, 64], P('seq', 'cfg')
Inputs may be any that keep to these rules, and one draw needn't show every extreme that they name: `tenant_lengths`: the lengths sum to 1280; the largest is exactly 960.
All inputs are finite; a program needn't handle non-finite values.
Results may differ from a plain program's by a relative error of at most 0.013.
Values may be sent and summed in bfloat16 or wider, within the bound.
A program may use at most 192 MiB of HBM per device.

v0:
```python
import math
import jax
import jax.numpy as jnp
from jax import lax
from jax.sharding import PartitionSpec as P

HD = 128
TEXT = 512
TENANTS = 4
epsilon = 1e-06


def partner_2(block, axis, distance):
    count = lax.axis_size(axis)
    route = []
    for low in range(count):
        high = low | 1 << distance
        if high != low and high < count:
            route += [(low, high), (high, low)]
    return lax.ppermute(block, axis, route)


def layer_norm(inputs):
    average = jnp.mean(inputs, axis=-1, keepdims=True)
    centred = inputs - average
    variance = jnp.mean(centred * centred, axis=-1, keepdims=True)
    return centred * lax.rsqrt(variance + epsilon)


def head_norm(inputs, head_dim):
    shaped = inputs.reshape(inputs.shape[:-1] + (inputs.shape[-1] // head_dim, head_dim))
    return shaped * lax.rsqrt(jnp.mean(shaped * shaped, axis=-1, keepdims=True) + epsilon)


def rotary(inputs, grid):
    head_dim = inputs.shape[-1]
    sixth_part = head_dim // 6
    angle_parts = []
    for dim_index, span_width in enumerate(
        (head_dim - 4 * sixth_part, 2 * sixth_part, 2 * sixth_part)
    ):
        exponent = jnp.arange(0, span_width, 2).astype(jnp.float32) / span_width
        frequency = 1.0 / 10000.0**exponent
        angle_parts.append(
            grid[:, dim_index : dim_index + 1].astype(jnp.float32) * frequency[None, :]
        )
    angles = jnp.concatenate(angle_parts, axis=1)[:, None, :]
    paired = inputs.reshape(inputs.shape[:-1] + (head_dim // 2, 2))
    even_part = paired[..., 0]
    odd_part = paired[..., 1]
    cosine = jnp.cos(angles)
    sinus = jnp.sin(angles)
    rotated = jnp.stack(
        [even_part * cosine - odd_part * sinus, even_part * sinus + odd_part * cosine], axis=-1
    )
    return rotated.reshape(inputs.shape)


def add_block(queries, keys, values, allowed):
    score_scale = 1.0 / math.sqrt(queries.shape[-1])
    scores = (
        jnp.einsum("qhd,khd->qhk", queries, keys, preferred_element_type=jnp.float32) * score_scale
    )
    weights = jnp.where(allowed[:, None, :], jnp.exp(scores), 0.0).astype(jnp.bfloat16)
    summed = jnp.einsum("qhk,khd->qhd", weights, values, preferred_element_type=jnp.float32)
    totals = jnp.sum(weights.astype(jnp.float32), axis=2)
    return (summed, totals)


def project_rows(normed, weight):
    return jnp.dot(
        normed,
        lax.all_gather(weight, ("cfg", "seq"), axis=0, tiled=True),
        preferred_element_type=jnp.float32,
    )


def project_out(mixed, weight):
    terms = lax.dot_general(
        mixed,
        lax.all_gather(weight, ("cfg", "seq"), axis=0, tiled=True),
        (((1,), (1,)), ((), ())),
        preferred_element_type=jnp.float32,
    )
    return lax.psum(terms.astype(jnp.bfloat16), "wt").astype(jnp.float32)


def on_device(
    hidden,
    latent,
    tenant_lengths,
    grid_positions,
    text_kv,
    text_lengths,
    w_query,
    w_key,
    w_value,
    w_out,
    w_cross_query,
    w_cross_out,
    w_head,
    guidance,
    step_size,
):
    tok_rows = hidden.shape[1]
    model_width = hidden.shape[2]
    local_cols = w_query.shape[1]
    heads_here = local_cols // HD
    seq_index = lax.axis_index("seq")
    ends = jnp.cumsum(tenant_lengths)

    def tenant_of(indices):
        return jnp.sum((indices[:, None] >= ends[None, :]).astype(jnp.int32), axis=1)

    my_tenant = tenant_of(seq_index * tok_rows + jnp.arange(tok_rows, dtype=jnp.int32))
    state = hidden[0].astype(jnp.float32)
    normed = layer_norm(state).astype(jnp.bfloat16)
    joined_weight = jnp.concatenate([w_query, w_key, w_value], axis=1)
    projected = project_rows(normed, joined_weight)
    queries = rotary(head_norm(projected[:, :local_cols], HD), grid_positions).astype(jnp.bfloat16)
    keys = rotary(head_norm(projected[:, local_cols : 2 * local_cols], HD), grid_positions).astype(
        jnp.bfloat16
    )
    keys = keys.reshape(tok_rows, local_cols)
    values = projected[:, 2 * local_cols :].astype(jnp.bfloat16)
    key_piece = lax.all_gather(keys, "seq", axis=0, tiled=True)
    value_piece = lax.all_gather(values, "seq", axis=0, tiled=True)
    piece_rows = key_piece.shape[0]
    key_tenant = tenant_of(jnp.arange(piece_rows, dtype=jnp.int32))
    allowed = my_tenant[:, None] == key_tenant[None, :]
    summed, totals = add_block(
        queries,
        key_piece.reshape(piece_rows, heads_here, HD),
        value_piece.reshape(piece_rows, heads_here, HD),
        allowed,
    )
    mixed = (summed / totals[..., None]).astype(jnp.bfloat16).reshape(tok_rows, local_cols)
    state = state + project_out(mixed, w_out)
    normed = layer_norm(state).astype(jnp.bfloat16)
    cross_queries = head_norm(project_rows(normed, w_cross_query), HD).astype(jnp.bfloat16)
    text_keys = head_norm(text_kv[0, 0].astype(jnp.float32), HD).astype(jnp.bfloat16)
    text_values = text_kv[1, 0].reshape(-1, heads_here, HD)
    text_index = jnp.arange(text_kv.shape[2], dtype=jnp.int32)
    text_tenant = text_index // TEXT
    text_slot = text_index % TEXT
    tenant_table = text_tenant[:, None] == jnp.arange(TENANTS, dtype=jnp.int32)[None, :]
    live_length = jnp.sum(jnp.where(tenant_table, text_lengths[0][None, :], 0), axis=1)
    allowed = (my_tenant[:, None] == text_tenant[None, :]) & (text_slot < live_length)[None, :]
    cross_summed, cross_totals = add_block(cross_queries, text_keys, text_values, allowed)
    cross_mixed = (
        (cross_summed / cross_totals[..., None]).astype(jnp.bfloat16).reshape(tok_rows, local_cols)
    )
    state = state + project_out(cross_mixed, w_cross_out)
    velocity = jnp.dot(
        layer_norm(state).astype(jnp.bfloat16), w_head, preferred_element_type=jnp.float32
    )
    half_index = lax.axis_index("cfg")
    channel_half = latent.shape[1]
    outgoing = lax.dynamic_slice_in_dim(velocity, (1 - half_index) * channel_half, channel_half, 1)
    partner = partner_2(outgoing, "cfg", 0)
    own_part = lax.dynamic_slice_in_dim(velocity, half_index * channel_half, channel_half, 1)
    conditional = jnp.where(half_index == 0, own_part, partner)
    null_text = jnp.where(half_index == 0, partner, own_part)
    latent_next = latent + step_size[0] * (null_text + guidance[0] * (conditional - null_text))
    slice_width = model_width // lax.axis_size("wt")
    hidden_out = lax.dynamic_slice_in_dim(
        state.astype(jnp.bfloat16), lax.axis_index("wt") * slice_width, slice_width, 1
    )
    return (hidden_out[None], latent_next)


def solution(mesh):
    return jax.shard_map(
        on_device,
        mesh=mesh,
        in_specs=(
            P("cfg", "seq", None),
            P("seq", "cfg"),
            P(),
            P("seq", None),
            P(None, "cfg", None, "wt"),
            P("cfg", None),
            P(("cfg", "seq"), "wt"),
            P(("cfg", "seq"), "wt"),
            P(("cfg", "seq"), "wt"),
            P(("cfg", "seq"), "wt"),
            P(("cfg", "seq"), "wt"),
            P(("cfg", "seq"), "wt"),
            P(),
            P(),
            P(),
        ),
        out_specs=(P("cfg", "seq", "wt"), P("seq", "cfg")),
        check_vma=False,
    )
```

profile of v0, /device:TPU:0, one launch (start us, length us, event | category | flops | bytes accessed | tf_op | source)
XLA Modules:
  0.0 949.5 jit_solution(14154485433411646982)
XLA Ops:
  7.2 3.7 pad_maximum_fusion
  12.4 233.7 %all-gather.7.cloned.1.call-done = bf16[5120,4608]{1,0:T(8,128)(2,1)} async-done(((bf16[320,4608]{1,0:T(8,128)(2,1)}), bf16[5120,4608]{1,0:T(8,128)(2,1)}) %all-gather.7.cloned.1.call-update) | async-done | bytes 47185936 | tf_op jit(solution)/shard_map/all_gather | solution.py:73
  246.1 20.1 %fusion.18 = f32[160,4608]{1,0:T(8,128)} fusion(bf16[5120,4608]{1,0:T(8,128)(2,1)} %all-gather.7.cloned.1.call-done, bf16[1,160,5120]{2,1,0:T(8,128)(2,1)S(1)} %copy-done.1, f32[160]{0:T(256)S(1)} %add_rsqrt_fusion.6, f32[160]{0:T(256)S(1)} %broadcast_multiply_fusion.7), kind=kOutput, calls=%fused_computation.31 | convolution fusion | flops 7553024000 | bytes 51774720 | tf_op jit(solution)/shard_map/dot_general | solution.py:71
  266.2 3.3 slice_multiply_fusion
  269.5 2.8 copy.72
  272.3 3.0 reshape.338
  275.3 2.8 copy.76
  278.2 3.0 reshape.340
  288.6 3.2 broadcast_multiply_fusion
  291.8 5.2 subtract_convert_fusion
  297.0 2.8 pad_maximum_fusion.1
  299.9 3.0 convert_element_type.123
  308.3 4.0 pad_maximum_fusion.2
  314.6 60.7 %all-gather.11.cloned.1.call-done = bf16[1280,1536]{1,0:T(8,128)(2,1)} async-done(((bf16[160,1536]{1,0:T(8,128)(2,1)}), bf16[1280,1536]{1,0:T(8,128)(2,1)}) %all-gather.11.cloned.1.call-update) | async-done | bytes 3932176 | tf_op jit(solution)/shard_map/all_gather | solution.py:126
  375.3 6.3 copy.75
  381.6 64.4 %all-gather.9.cloned.1.call-done = bf16[1280,1536]{1,0:T(8,128)(2,1)} async-done(((bf16[160,1536]{1,0:T(8,128)(2,1)}), bf16[1280,1536]{1,0:T(8,128)(2,1)}) %all-gather.9.cloned.1.call-update) | async-done | bytes 3932176 | tf_op jit(solution)/shard_map/all_gather | solution.py:127
  445.9 6.2 copy.71
  452.1 5.6 convert_reduce_fusion.1
  459.2 107.6 %all-gather.13.cloned.1.call-done = bf16[5120,1536]{1,0:T(8,128)(2,1)} async-done(((bf16[320,1536]{1,0:T(8,128)(2,1)}), bf16[5120,1536]{1,0:T(8,128)(2,1)}) %all-gather.13.cloned.1.call-update) | async-done | bytes 15728656 | tf_op jit(solution)/shard_map/all_gather | solution.py:81
  566.7 11.9 %convolution_convert_fusion.1 = bf16[160,5120]{1,0:T(8,128)(2,1)} fusion(bf16[5120,1536]{1,0:T(8,128)(2,1)} %all-gather.13.cloned.1.call-done, bf16[12,20,8,128]{3,2,1,0:T(8,128)(2,1)S(1)} %fusion.28), kind=kOutput, calls=%fused_computation.13 | convolution fusion | flops 2517401600 | bytes 17858560 | tf_op jit(solution)/shard_map/dot_general | solution.py:79
  580.0 10.6 %fusion.47 = (bf16[1,1,2048,1536]{3,2,1,0:T(8,128)(2,1)}, bf16[1,1,2048,1536]{3,2,1,0:T(8,128)(2,1)}) fusion(bf16[2,1,2048,1536]{3,2,1,0:T(8,128)(2,1)} %param.19), kind=kLoop, calls=%fused_computation.109 | loop fusion | bytes 25165824 | tf_op jit(solution)/shard_map/slice | solution.py:142
  590.6 8.7 copy.95
  599.4 8.8 copy.96
  608.3 4.7 fusion.1
  614.0 15.8 %all-reduce.3.cloned.1.call-done = bf16[160,5120]{1,0:T(8,128)(2,1)} async-done(((bf16[160,5120]{1,0:T(8,128)(2,1)}), bf16[160,5120]{1,0:T(8,128)(2,1)}) %all-reduce.3.cloned.1.call-update) | async-done | bytes 1638416 | tf_op jit(solution)/shard_map/psum | solution.py:85
  632.7 119.8 %all-gather.15.cloned.1.call-done = bf16[5120,1536]{1,0:T(8,128)(2,1)} async-done(((bf16[320,1536]{1,0:T(8,128)(2,1)}), bf16[5120,1536]{1,0:T(8,128)(2,1)}) %all-gather.15.cloned.1.call-update) | async-done | bytes 15728656 | tf_op jit(solution)/shard_map/all_gather | solution.py:73
  752.5 7.6 fusion.16
  765.3 7.7 convert_reduce_fusion
  775.3 98.3 %all-gather.17.cloned.1.call-done = bf16[5120,1536]{1,0:T(8,128)(2,1)} async-done(((bf16[320,1536]{1,0:T(8,128)(2,1)}), bf16[5120,1536]{1,0:T(8,128)(2,1)}) %all-gather.17.cloned.1.call-update) | async-done | bytes 15728656 | tf_op jit(solution)/shard_map/all_gather | solution.py:81
  873.5 11.9 %convolution_convert_fusion = bf16[160,5120]{1,0:T(8,128)(2,1)} fusion(bf16[5120,1536]{1,0:T(8,128)(2,1)} %all-gather.17.cloned.1.call-done, bf16[12,20,8,128]{3,2,1,0:T(8,128)(2,1)S(1)} %fusion.29), kind=kOutput, calls=%fused_computation.12 | convolution fusion | flops 2517401600 | bytes 17858560 | tf_op jit(solution)/shard_map/dot_general | solution.py:79
  886.7 49.9 %all-reduce.5.cloned.1.call-done = bf16[160,5120]{1,0:T(8,128)(2,1)} async-done(((bf16[160,5120]{1,0:T(8,128)(2,1)}), bf16[160,5120]{1,0:T(8,128)(2,1)}) %all-reduce.5.cloned.1.call-update) | async-done | bytes 1638416 | tf_op jit(solution)/shard_map/psum | solution.py:85
  936.7 2.6 fusion.46
  (91 shorter events, 33.8 us)
Async XLA Ops:
  7.2 932.6 %copy-start = (bf16[5120,64]{0,1:T(8,128)(2,1)S(1)}, bf16[5120,64]{0,1:T(8,128)(2,1)}, u32[]{:S(2)}) copy-start(bf16[5120,64]{0,1:T(8,128)(2,1)} %param.27) | copy-start | bytes 1966084
  7.2 3.9 copy-start.6
  7.2 4.3 copy-start.1
  7.2 238.9 %all-gather.7.cloned.1.call-start = ((), (), s32[]{:S(2)}) async-start(), calls=%async_computation | async-start | bytes 50135040 | tf_op jit(solution)/shard_map/all_gather | solution.py:73
  11.0 364.3 %all-gather.11.cloned.1.call-start = ((), (), s32[]{:S(2)}) async-start(), calls=%async_computation.2 | async-start | bytes 4423680 | tf_op jit(solution)/shard_map/all_gather | solution.py:126
  299.9 7.9 copy-start.8
  305.0 140.9 %all-gather.9.cloned.1.call-start = ((), (), s32[]{:S(2)}) async-start(), calls=%async_computation.1 | async-start | bytes 4423680 | tf_op jit(solution)/shard_map/all_gather | solution.py:127
  307.1 259.6 %all-gather.13.cloned.1.call-start = ((), (), s32[]{:S(2)}) async-start(), calls=%async_computation.3 | async-start | bytes 16711680 | tf_op jit(solution)/shard_map/all_gather | solution.py:81
  307.7 322.1 %all-reduce.3.cloned.1.call-start = ((), (), s32[]{:S(2)}) async-start(), calls=%async_computation.4 | async-start | bytes 3276800 | tf_op jit(solution)/shard_map/psum | solution.py:85
  452.1 5.6 copy-start.3
  578.6 173.9 %all-gather.15.cloned.1.call-start = ((), (), s32[]{:S(2)}) async-start(), calls=%async_computation.5 | async-start | bytes 16711680 | tf_op jit(solution)/shard_map/all_gather | solution.py:73
  579.2 294.3 %all-gather.17.cloned.1.call-start = ((), (), s32[]{:S(2)}) async-start(), calls=%async_computation.6 | async-start | bytes 16711680 | tf_op jit(solution)/shard_map/all_gather | solution.py:81
  580.0 356.7 %all-reduce.5.cloned.1.call-start = ((), (), s32[]{:S(2)}) async-start(), calls=%async_computation.7 | async-start | bytes 3276800 | tf_op jit(solution)/shard_map/psum | solution.py:85
  599.4 8.8 copy-start.7
  629.9 2.1 copy-start.2
  761.3 4.0 copy-start.4
  763.4 9.6 %slice-start = ((s8[6291456]{0:T(1024)(128)(4,1)}), s8[4194304]{0:T(1024)(128)(4,1)S(1)}, s32[]{:S(2)}) async-start(s8[6291456]{0:T(1024)(128)(4,1)} %bitcast.95), calls=%async_computation.8 | async-start | bytes 8388608
  765.3 7.7 slice-start.1
  939.8 2.1 copy-start.5
  940.6 1.3 collective-permute-start
Sparse Core Ops, SparseCore 0:
  11.1 234.9 all-gather.6
  305.1 70.0 all-gather.10
  377.5 68.4 all-gather.8
  448.0 118.6 all-gather.12
  578.7 51.0 all-reduce.2
  632.2 120.2 all-gather.14
  755.0 118.4 all-gather.16
  885.5 51.0 all-reduce.4
where the time goes:
time: 959 us; the launch traced here: 950 us
  waiting for transfers between devices  752 us (78%)
  matrix products  69 us (7%)
  local copies, waits for them, and re-layouts  68.1 us (7%)
  other arithmetic  43.8 us (5%)
  between operations  16 us (2%)
    all_gather x2, waiting for transfers between devices, project_rows(): lax.all_gather(weight, ('cfg', 'seq'), axis=0, tiled=True)  354 us
    all_gather x2, waiting for transfers between devices, project_out(): lax.all_gather(weight, ('cfg', 'seq'), axis=0, tiled=True)  206 us
    psum x2, waiting for transfers between devices, project_out(): return lax.psum(terms.astype(jnp.bfloat16), 'wt').astype(jnp.float32)  65.8 us
    all_gather x1, waiting for transfers between devices, on_device(): value_piece = lax.all_gather(values, 'seq', axis=0, tiled=True)  64.4 us
    all_gather x1, waiting for transfers between devices, on_device(): key_piece = lax.all_gather(keys, 'seq', axis=0, tiled=True)  60.7 us
    dot_general x2, matrix products, project_rows(): jnp.dot(normed, lax.all_gather(weight, ('cfg', 'seq'), axis=0, tiled=True...  27.7 us
    dot_general x2, matrix products, project_out(): lax.dot_general(mixed, lax.all_gather(weight, ('cfg', 'seq'), axis=0, til...  23.7 us
  transfers between devices with their start and end apart: 9, of which 9 were waited for; matrix products, arithmetic and copies ran while one was open for 9% of the time, Pallas kernels for 0%

commit v1 on v0

--- a/solution.py
+++ b/solution.py
@@ -3,6 +3,7 @@
 import jax.numpy as jnp
 from jax import lax
 from jax.sharding import PartitionSpec as P
+from jax.lax import axis_index, ppermute, psum
 
 HD = 128
 TEXT = 512
@@ -102,6 +103,29 @@
     guidance,
     step_size,
 ):
+
+    def rest_blocks(inp):
+        b_next = psum(1, axis_name="seq")
+        r1, y, side_arr = (b_next, axis_index("seq"), inp.shape[0])
+        row_out = lax.dynamic_update_slice_in_dim(
+            jnp.zeros([at * r1 if num == 0 else at for num, at in enumerate(inp.shape)], inp.dtype),
+            inp,
+            y * side_arr,
+            axis=0,
+        )
+        w2 = everything = inp
+        for i0 in range(1, r1 // 2 + 1):
+            w2 = ppermute(w2, "seq", list(map(lambda num: (num, (num + 1) % r1), range(r1))))
+            row_out = lax.dynamic_update_slice_in_dim(row_out, w2, (y - i0) % r1 * side_arr, axis=0)
+            if 2 * i0 < r1:
+                everything = ppermute(
+                    everything, "seq", perm=list(map(lambda num: (num, (num - 1) % r1), range(r1)))
+                )
+                row_out = lax.dynamic_update_slice_in_dim(
+                    row_out, everything, (y + i0) % r1 * side_arr, axis=0
+                )
+        return row_out
+
     tok_rows = hidden.shape[1]
     model_width = hidden.shape[2]
     local_cols = w_query.shape[1]
@@ -123,7 +147,7 @@
     )
     keys = keys.reshape(tok_rows, local_cols)
     values = projected[:, 2 * local_cols :].astype(jnp.bfloat16)
-    key_piece = lax.all_gather(keys, "seq", axis=0, tiled=True)
+    key_piece = rest_blocks(keys)
     value_piece = lax.all_gather(values, "seq", axis=0, tiled=True)
     piece_rows = key_piece.shape[0]
     key_tenant = tenant_of(jnp.arange(piece_rows, dtype=jnp.int32))

time: 959 us -> 895 us (0.933)
  waiting for transfers between devices: 752 us -> 596 us
  local copies, waits for them, and re-layouts: 68.1 us -> 141 us
  starting transfers between devices: 0.39 us -> 17.1 us
    all_gather x2, waiting for transfers between devices: 206 us -> 117 us  [project_out(): lax.all_gather(weight, ('cfg', 'seq'), axis=0, tiled=True)]
    dynamic_update_slice x0 -> x8, local copies, waits for them, and re-layouts: none -> 68.3 us  [the longest x4 33.7 us: rest_blocks(): lax.dynamic_update_slice_in_dim(row_out, w2, (y - i0) % r1 * side_arr, ax...]
    all_gather x1, waiting for transfers between devices: 64.4 us -> 0.01 us  [on_device(): value_piece = lax.all_gather(values, 'seq', axis=0, tiled=True)]
    all_gather x1 -> x0, waiting for transfers between devices: 60.7 us -> none  [on_device(): key_piece = lax.all_gather(keys, 'seq', axis=0, tiled=True)]
    ppermute x0 -> x7, waiting for transfers between devices: none -> 54.2 us  [the longest x4 54.2 us: rest_blocks(): ppermute(w2, 'seq', list(map(lambda num: (num, (num + 1) % r1), range(r1))))]
    ppermute x0 -> x7, starting transfers between devices: none -> 16.5 us  [the longest x3 11.3 us: rest_blocks(): ppermute(everything, 'seq', perm=list(map(lambda num: (num, (num - 1) % r...]
  transfers between devices with their start and end apart: 9 -> 15, of which waited for: 9 -> 10; matrix products, arithmetic and copies ran while one was open for 9% -> 23% of each run, Pallas kernels for 0% -> 0%
where the time goes in v1:
time: 895 us; the launch traced here: 888 us
  waiting for transfers between devices  596 us (67%)
  local copies, waits for them, and re-layouts  141 us (16%)
  matrix products  74.5 us (8%)
  other arithmetic  43.7 us (5%)
  starting transfers between devices  17.1 us (2%)
  between operations  16 us (2%)
    all_gather x2, waiting for transfers between devices, project_rows(): lax.all_gather(weight, ('cfg', 'seq'), axis=0, tiled=True)  354 us
    all_gather x2, waiting for transfers between devices, project_out(): lax.all_gather(weight, ('cfg', 'seq'), axis=0, tiled=True)  117 us
    psum x2, waiting for transfers between devices, project_out(): return lax.psum(terms.astype(jnp.bfloat16), 'wt').astype(jnp.float32)  69 us
    ppermute x4, waiting for transfers between devices, rest_blocks(): ppermute(w2, 'seq', list(map(lambda num: (num, (num + 1) % r1), range(r1))))  54.2 us
    dynamic_update_slice x4, local copies, waits for them, and re-layouts, rest_blocks(): lax.dynamic_update_slice_in_dim(row_out, w2, (y - i0) % r1 * side_arr, ax...  33.7 us
    dot_general x2, matrix products, project_rows(): jnp.dot(normed, lax.all_gather(weight, ('cfg', 'seq'), axis=0, tiled=True...  27.6 us
    dynamic_update_slice x3, local copies, waits for them, and re-layouts, rest_blocks(): lax.dynamic_update_slice_in_dim(row_out, everything, (y + i0) % r1 * side...  26.7 us
    dot_general x2, matrix products, project_out(): lax.dot_general(mixed, lax.all_gather(weight, ('cfg', 'seq'), axis=0, til...  23.7 us
  transfers between devices with their start and end apart: 15, of which 10 were waited for; matrix products, arithmetic and copies ran while one was open for 23% of the time, Pallas kernels for 0%

profile of v1, /device:TPU:0, one launch (start us, length us, event | category | flops | bytes accessed | tf_op | source)
XLA Modules:
  0.0 888.5 jit_solution(15406728507043232936)
XLA Ops:
  12.0 234.1 %all-gather.6.cloned.1.call-done = bf16[5120,4608]{1,0:T(8,128)(2,1)} async-done(((bf16[320,4608]{1,0:T(8,128)(2,1)}), bf16[5120,4608]{1,0:T(8,128)(2,1)}) %all-gather.6.cloned.1.call-update) | async-done | bytes 47185936 | tf_op jit(solution)/shard_map/all_gather | solution.py:74
  246.1 20.1 %fusion.18 = f32[160,4608]{1,0:T(8,128)} fusion(bf16[5120,4608]{1,0:T(8,128)(2,1)} %all-gather.6.cloned.1.call-done, bf16[1,160,5120]{2,1,0:T(8,128)(2,1)S(1)} %copy-done.1, f32[160]{0:T(256)S(1)} %add_rsqrt_fusion.6, f32[160]{0:T(256)S(1)} %broadcast_multiply_fusion.7), kind=kOutput, calls=%fused_computation.31 | convolution fusion | flops 7553024000 | bytes 51774720 | tf_op jit(solution)/shard_map/dot_general | solution.py:72
  295.6 5.1 subtract_convert_fusion
  311.5 29.0 %collective-permute-done = bf16[160,1536]{1,0:T(8,128)(2,1)S(1)} collective-permute-done((bf16[160,1536]{1,0:T(8,128)(2,1)}, bf16[160,1536]{1,0:T(8,128)(2,1)S(1)}, u32[]{:S(2)}, u32[]{:S(2)}) %collective-permute-start) | collective-permute-done | bytes 491552 | tf_op jit(solution)/shard_map/ppermute | solution.py:118
  346.0 19.2 %collective-permute-done.2 = bf16[160,1536]{1,0:T(8,128)(2,1)} collective-permute-done((bf16[160,1536]{1,0:T(8,128)(2,1)S(1)}, bf16[160,1536]{1,0:T(8,128)(2,1)}, u32[]{:S(2)}, u32[]{:S(2)}) %collective-permute-start.2) | collective-permute-done | bytes 491552 | tf_op jit(solution)/shard_map/ppermute | solution.py:118
  367.0 5.2 collective-permute-start.5
  372.2 6.0 collective-permute-done.4
  378.9 4.4 pad_maximum_fusion.2
  388.4 7.9 dynamic_update_slice.24
  397.6 8.2 dynamic_update_slice.25
  407.1 8.9 dynamic_update_slice.26
  417.3 8.7 dynamic_update_slice.27
  427.3 9.0 %dynamic_update_slice.28 = bf16[1280,1536]{0,1:T(8,128)(2,1)} dynamic-update-slice(bf16[1280,1536]{0,1:T(8,128)(2,1)} %dynamic_update_slice.27, bf16[160,1536]{0,1:T(8,128)(2,1)S(1)} %copy.93, s32[]{:T(128)S(6)} %select_n.121, s32[]{:T(128)} %constant.124.clone.1) | dynamic-update-slice | bytes 983044 | tf_op jit(solution)/shard_map/dynamic_update_slice | solution.py:124
  437.5 8.9 %dynamic_update_slice.29 = bf16[1280,1536]{0,1:T(8,128)(2,1)} dynamic-update-slice(bf16[1280,1536]{0,1:T(8,128)(2,1)} %dynamic_update_slice.28, bf16[160,1536]{0,1:T(8,128)(2,1)S(1)} %copy.94, s32[]{:T(128)S(6)} %select_n.123, s32[]{:T(128)} %constant.124.clone.1) | dynamic-update-slice | bytes 983044 | tf_op jit(solution)/shard_map/dynamic_update_slice | solution.py:119
  447.8 8.8 dynamic_update_slice.30
  457.9 8.0 dynamic_update_slice.31
  465.9 7.5 convert_reduce_fusion.1
  473.4 6.5 copy.85
  480.0 5.0 fusion.28
  485.0 18.4 %all-gather.10.cloned.1.call-done = bf16[5120,1536]{1,0:T(8,128)(2,1)} async-done(((bf16[320,1536]{1,0:T(8,128)(2,1)}), bf16[5120,1536]{1,0:T(8,128)(2,1)}) %all-gather.10.cloned.1.call-update) | async-done | bytes 15728656 | tf_op jit(solution)/shard_map/all_gather | solution.py:82
  503.4 11.9 %convolution_convert_fusion.1 = bf16[160,5120]{1,0:T(8,128)(2,1)} fusion(bf16[5120,1536]{1,0:T(8,128)(2,1)} %all-gather.10.cloned.1.call-done, bf16[12,20,8,128]{3,2,1,0:T(8,128)(2,1)S(1)} %fusion.28), kind=kOutput, calls=%fused_computation.13 | convolution fusion | flops 2517401600 | bytes 17858560 | tf_op jit(solution)/shard_map/dot_general | solution.py:80
  516.5 10.3 %fusion.47 = (bf16[1,1,2048,1536]{3,2,1,0:T(8,128)(2,1)}, bf16[1,1,2048,1536]{3,2,1,0:T(8,128)(2,1)}) fusion(bf16[2,1,2048,1536]{3,2,1,0:T(8,128)(2,1)} %param.19), kind=kLoop, calls=%fused_computation.109 | loop fusion | bytes 25165824 | tf_op jit(solution)/shard_map/slice | solution.py:166
  526.9 8.7 copy.116
  535.6 8.8 copy.117
  544.6 4.3 fusion.1
  549.9 19.1 %all-reduce.3.cloned.1.call-done = bf16[160,5120]{1,0:T(8,128)(2,1)} async-done(((bf16[160,5120]{1,0:T(8,128)(2,1)}), bf16[160,5120]{1,0:T(8,128)(2,1)}) %all-reduce.3.cloned.1.call-update) | async-done | bytes 1638416 | tf_op jit(solution)/shard_map/psum | solution.py:86
  571.8 119.8 %all-gather.12.cloned.1.call-done = bf16[5120,1536]{1,0:T(8,128)(2,1)} async-done(((bf16[320,1536]{1,0:T(8,128)(2,1)}), bf16[5120,1536]{1,0:T(8,128)(2,1)}) %all-gather.12.cloned.1.call-update) | async-done | bytes 15728656 | tf_op jit(solution)/shard_map/all_gather | solution.py:74
  691.6 7.6 fusion.16
  704.4 7.7 convert_reduce_fusion
  714.3 98.2 %all-gather.14.cloned.1.call-done = bf16[5120,1536]{1,0:T(8,128)(2,1)} async-done(((bf16[320,1536]{1,0:T(8,128)(2,1)}), bf16[5120,1536]{1,0:T(8,128)(2,1)}) %all-gather.14.cloned.1.call-update) | async-done | bytes 15728656 | tf_op jit(solution)/shard_map/all_gather | solution.py:82
  812.4 11.9 %convolution_convert_fusion = bf16[160,5120]{1,0:T(8,128)(2,1)} fusion(bf16[5120,1536]{1,0:T(8,128)(2,1)} %all-gather.14.cloned.1.call-done, bf16[12,20,8,128]{3,2,1,0:T(8,128)(2,1)S(1)} %fusion.29), kind=kOutput, calls=%fused_computation.12 | convolution fusion | flops 2517401600 | bytes 17858560 | tf_op jit(solution)/shard_map/dot_general | solution.py:80
  825.6 49.9 %all-reduce.5.cloned.1.call-done = bf16[160,5120]{1,0:T(8,128)(2,1)} async-done(((bf16[160,5120]{1,0:T(8,128)(2,1)}), bf16[160,5120]{1,0:T(8,128)(2,1)}) %all-reduce.5.cloned.1.call-update) | async-done | bytes 1638416 | tf_op jit(solution)/shard_map/psum | solution.py:86
  (117 shorter events, 85.4 us)
Async XLA Ops:
  7.2 871.6 %copy-start = (bf16[5120,64]{0,1:T(8,128)(2,1)S(1)}, bf16[5120,64]{0,1:T(8,128)(2,1)}, u32[]{:S(2)}) copy-start(bf16[5120,64]{0,1:T(8,128)(2,1)} %param.27) | copy-start | bytes 1966084
  7.2 3.9 copy-start.1
  7.2 238.9 %all-gather.6.cloned.1.call-start = ((), (), s32[]{:S(2)}) async-start(), calls=%async_computation | async-start | bytes 50135040 | tf_op jit(solution)/shard_map/all_gather | solution.py:74
  11.0 462.4 %all-gather.8.cloned.1.call-start = ((), (), s32[]{:S(2)}) async-start(), calls=%async_computation.1 | async-start | bytes 4423680 | tf_op jit(solution)/shard_map/all_gather | solution.py:151
  12.0 257.3 %copy-start.6 = (s32[160,3]{0,1:T(4,128)S(1)}, s32[160,3]{0,1:T(4,128)}, u32[]{:S(2)}) copy-start(s32[160,3]{0,1:T(4,128)} %param.18) | copy-start | bytes 5764
  268.2 235.2 %all-gather.10.cloned.1.call-start = ((), (), s32[]{:S(2)}) async-start(), calls=%async_computation.2 | async-start | bytes 16711680 | tf_op jit(solution)/shard_map/all_gather | solution.py:82
  269.0 300.0 %all-reduce.3.cloned.1.call-start = ((), (), s32[]{:S(2)}) async-start(), calls=%async_computation.3 | async-start | bytes 3276800 | tf_op jit(solution)/shard_map/psum | solution.py:86
  300.6 66.0 %copy-start.8 = (s32[4]{0:T(128)S(1)}, s32[4]{0:T(128)}, u32[]{:S(2)}) copy-start(s32[4]{0:T(128)} %param.17) | copy-start | bytes 52
  306.8 33.7 %collective-permute-start = (bf16[160,1536]{1,0:T(8,128)(2,1)}, bf16[160,1536]{1,0:T(8,128)(2,1)S(1)}, u32[]{:S(2)}, u32[]{:S(2)}) collective-permute-start(bf16[160,1536]{1,0:T(8,128)(2,1)} %copy.88), channel_id=1, source_target_pairs={{0,2},{2,4},{4,6},{6,8},{8,10},{10,12},{12,14},{14,0},{1,3},{3,5},... | collective-permute-start | bytes 1474568 | tf_op jit(solution)/shard_map/ppermute | solution.py:118
  307.7 35.9 %collective-permute-start.1 = (bf16[160,1536]{1,0:T(8,128)(2,1)}, bf16[160,1536]{1,0:T(8,128)(2,1)}, u32[]{:S(2)}, u32[]{:S(2)}) collective-permute-start(bf16[160,1536]{1,0:T(8,128)(2,1)} %copy.88), channel_id=1, source_target_pairs={{0,14},{2,0},{4,2},{6,4},{8,6},{10,8},{12,10},{14,12},{1,15},{3,1}... | collective-permute-start | bytes 1474568 | tf_op jit(solution)/shard_map/ppermute | solution.py:121
  340.5 0.8 copy-start.3
  341.3 23.9 %collective-permute-start.2 = (bf16[160,1536]{1,0:T(8,128)(2,1)S(1)}, bf16[160,1536]{1,0:T(8,128)(2,1)}, u32[]{:S(2)}, u32[]{:S(2)}) collective-permute-start(bf16[160,1536]{1,0:T(8,128)(2,1)S(1)} %collective-permute-done), channel_id=1, source_target_pairs={{0,2},{2,4},{4,6},{6,8},{8,10},{10,12},{12,14},{14,0},{1,3},{3,5},... | collective-permute-start | bytes 1474568 | tf_op jit(solution)/shard_map/ppermute | solution.py:118
  343.6 23.3 %collective-permute-start.3 = (bf16[160,1536]{1,0:T(8,128)(2,1)}, bf16[160,1536]{1,0:T(8,128)(2,1)}, u32[]{:S(2)}, u32[]{:S(2)}) collective-permute-start(bf16[160,1536]{1,0:T(8,128)(2,1)} %collective-permute-done.1), channel_id=1, source_target_pairs={{0,14},{2,0},{4,2},{6,4},{8,6},{10,8},{12,10},{14,12},{1,15},{3,1}... | collective-permute-start | bytes 1474568 | tf_op jit(solution)/shard_map/ppermute | solution.py:121
  365.2 13.1 %collective-permute-start.4 = (bf16[160,1536]{1,0:T(8,128)(2,1)}, bf16[160,1536]{1,0:T(8,128)(2,1)}, u32[]{:S(2)}, u32[]{:S(2)}) collective-permute-start(bf16[160,1536]{1,0:T(8,128)(2,1)} %collective-permute-done.2), channel_id=1, source_target_pairs={{0,2},{2,4},{4,6},{6,8},{8,10},{10,12},{12,14},{14,0},{1,3},{3,5},... | collective-permute-start | bytes 1474568 | tf_op jit(solution)/shard_map/ppermute | solution.py:118
  367.0 79.5 %collective-permute-start.5 = (bf16[160,1536]{1,0:T(8,128)(2,1)}, bf16[160,1536]{1,0:T(8,128)(2,1)}, u32[]{:S(2)}, u32[]{:S(2)}) collective-permute-start(bf16[160,1536]{1,0:T(8,128)(2,1)} %collective-permute-done.3), channel_id=1, source_target_pairs={{0,14},{2,0},{4,2},{6,4},{8,6},{10,8},{12,10},{14,12},{1,15},{3,1}... | collective-permute-start | bytes 1474568 | tf_op jit(solution)/shard_map/ppermute | solution.py:121
  378.3 78.4 %collective-permute-start.6 = (bf16[160,1536]{1,0:T(8,128)(2,1)}, bf16[160,1536]{1,0:T(8,128)(2,1)}, u32[]{:S(2)}, u32[]{:S(2)}) collective-permute-start(bf16[160,1536]{1,0:T(8,128)(2,1)} %collective-permute-done.4), channel_id=1, source_target_pairs={{0,2},{2,4},{4,6},{6,8},{8,10},{10,12},{12,14},{14,0},{1,3},{3,5},... | collective-permute-start | bytes 1474568 | tf_op jit(solution)/shard_map/ppermute | solution.py:118
  515.3 176.3 %all-gather.12.cloned.1.call-start = ((), (), s32[]{:S(2)}) async-start(), calls=%async_computation.4 | async-start | bytes 16711680 | tf_op jit(solution)/shard_map/all_gather | solution.py:74
  515.9 296.5 %all-gather.14.cloned.1.call-start = ((), (), s32[]{:S(2)}) async-start(), calls=%async_computation.5 | async-start | bytes 16711680 | tf_op jit(solution)/shard_map/all_gather | solution.py:82
  516.5 359.1 %all-reduce.5.cloned.1.call-start = ((), (), s32[]{:S(2)}) async-start(), calls=%async_computation.6 | async-start | bytes 3276800 | tf_op jit(solution)/shard_map/psum | solution.py:86
  535.6 8.8 copy-start.7
  568.9 2.1 copy-start.2
  700.4 4.0 copy-start.4
  702.5 9.6 %slice-start = ((s8[6291456]{0:T(1024)(128)(4,1)}), s8[4194304]{0:T(1024)(128)(4,1)S(1)}, s32[]{:S(2)}) async-start(s8[6291456]{0:T(1024)(128)(4,1)} %bitcast.95), calls=%async_computation.7 | async-start | bytes 8388608
  704.4 7.7 slice-start.1
  878.7 2.1 copy-start.5
  879.5 1.3 collective-permute-start.7
Sparse Core Ops, SparseCore 0:
  11.1 234.9 all-gather.5
  268.4 99.4 all-gather.7
  370.1 133.2 all-gather.9
  515.5 53.4 all-reduce.2
  571.3 120.2 all-gather.11
  693.9 118.4 all-gather.13
  824.4 51.0 all-reduce.4
